TPU v7x, 512 devices: a whole 4x4x16 slice. The times are simulated.
512 devices in a mesh: pts: 64 (over x, z), cand: 8 (over y, core).
Axes of the slice: x: 4, y: 4, z: 16, core: 2. Of those that a mesh axis runs over, the one named last changes fastest.
Arguments:
- points: bfloat16 [32768, 4096], P('pts'), may hold values from -6 to 6
- weights: float32 [32768], P('pts'), may hold values from 0.25 to 4
- coverage: float32 [32768], P('pts'), may hold values from 0 to 1.5
- cand_index: int32 [2, 4096], P(None, 'pts'), may hold values from 0 to 511
- winners: int32 [2], replicated, may hold values from 0 to 4095
Outputs:
- gains: float32 [2, 4096], P(None, ('pts', 'cand'))
- final_cover: float32 [32768], P('pts')
All inputs are finite; a program needn't handle non-finite values.
Results may differ from a plain program's by a relative error of at most 0.0003.
Values may be sent and summed in bfloat16 or wider, within the bound.
No kernel may reach another device: no remote copies, remote signals or barrier semaphores. Data moves between devices by JAX's collectives and lax.ppermute only.
A program may use at most 64 MiB of HBM per device.

v0:
```python
import jax
import jax.numpy as jnp
from jax import lax
from jax.sharding import Mesh
from jax.sharding import PartitionSpec as P

PTS = ("pts_0", "pts_1")
PTS_CAND = ("pts_0", "pts_1", "cand")
LIFT = 2.0**13


def body(points, weights, coverage, cand_index, winners):
    rows_dev, width = points.shape
    steps, per_row = cand_index.shape
    n_x, n_z = (lax.axis_size(axis) for axis in PTS)
    n_cand = lax.axis_size("cand")
    per_dev = per_row // n_cand
    held = steps * per_dev
    total = float(rows_dev * n_x * n_z)
    scale = width ** (-0.5) / LIFT
    my_cand = lax.axis_index("cand")
    my_pts = lax.axis_index(PTS)
    mine = lax.dynamic_slice_in_dim(cand_index, my_cand * per_dev, per_dev, 1).reshape(-1)
    owner = winners // per_row
    won = jnp.take_along_axis(cand_index, (winners % per_row)[:, None], axis=1)[:, 0]
    won = jnp.where(owner == my_pts, won, -1)
    wanted = jnp.concatenate([mine, won])
    pick = jnp.where(
        wanted[:, None] == lax.broadcasted_iota(jnp.int32, (held + steps, rows_dev), 1), LIFT, 0.0
    ).astype(points.dtype)
    picked = lax.dot_general(
        pick, points, (((1,), (0,)), ((), ())), preferred_element_type=jnp.float32
    ).astype(jnp.float16)
    piece = steps * width // held
    sent = jnp.concatenate([picked[:held], picked[held:].reshape(held, piece)], axis=1)
    along_z = lax.all_gather(sent, PTS[1], axis=0, tiled=True)
    owner_x, owner_z = (owner // n_z, owner % n_z)
    part = held // steps
    chosen = [
        lax.dynamic_slice(along_z, (owner_z[t] * held + t * part, width), (part, piece)).reshape(
            1, width
        )
        for t in range(steps)
    ]
    pad = jnp.zeros((8 - steps, width), jnp.float16)
    column = jnp.concatenate([along_z[:, :width], *chosen, pad], axis=0)
    column_rows = n_z * held + 8
    block = lax.all_gather(column, PTS[0], axis=0, tiled=True).astype(points.dtype)
    block = block.reshape(n_x, column_rows, width)
    chosen = jnp.concatenate(
        [
            lax.dynamic_slice(block, (owner_x[t], n_z * held + t, 0), (1, 1, width))[0]
            for t in range(steps)
        ]
    )
    near = (
        lax.dot_general(
            points, chosen, (((1,), (1,)), ((), ())), preferred_element_type=jnp.float32
        )
        * scale
    )
    covers = [coverage]
    for t in range(steps):
        covers.append(jnp.maximum(covers[-1], near[:, t]))
    step_of = lax.broadcasted_iota(jnp.int32, (1, 1, n_z * held), 2) % held // per_dev
    cover = covers[0][:, None, None]
    for t in range(1, steps):
        cover = jnp.where(step_of >= t, covers[t][:, None, None], cover)
    sim = (
        lax.dot_general(
            points,
            block[:, : n_z * held],
            (((1,), (2,)), ((), ())),
            preferred_element_type=jnp.float32,
        )
        * scale
    )
    part = jnp.sum(weights[:, None, None] * jnp.maximum(sim - cover, 0.0), axis=0)
    part = lax.all_to_all(part.reshape(n_x * n_z, held), PTS, 0, 0, tiled=True)
    gains = jnp.sum(part, axis=0) / total
    return (gains.reshape(steps, per_dev), covers[-1])


def solution(mesh):
    torus = Mesh(mesh.devices.reshape(4, 16, mesh.shape["cand"]), ("pts_0", "pts_1", "cand"))
    in_specs = (P(PTS, None), P(PTS), P(PTS), P(None, PTS), P())
    out_specs = (P(None, PTS_CAND), P(PTS))
    return jax.shard_map(body, mesh=torus, in_specs=in_specs, out_specs=out_specs, check_vma=False)
```

profile of v0, /device:TPU:24, one launch (start us, length us, event | category | flops | bytes accessed | tf_op | source)
XLA Modules:
  0.0 183.7 jit_solution(2298904888433843876)
XLA Ops:
  0.7 0.7 and_select_fusion
  1.4 0.1 copy.9
  1.4 0.2 or_reduce_fusion
  1.6 0.6 gather_fusion
  2.4 0.1 reshape.151
  2.4 0.1 pad_add_fusion.1
  2.5 2.9 %convolution_convert_fusion = f16[18,4096]{1,0:T(8,128)(2,1)S(1)} fusion(bf16[512,4096]{1,0:T(8,128)(2,1)} %param.5, s32[18]{0:T(128)S(1)} %pad_add_fusion.1), kind=kOutput, calls=%fused_computation.3 | convolution fusion | flops 75598848 | bytes 4341832 | tf_op jit(solution)/shard_map/dot_general | solution.py:31
  5.5 0.6 fusion.23
  8.6 51.8 %all-gather.2 = f16[256,4608]{1,0:T(8,128)(2,1)S(1)} all-gather(f16[16,4608]{1,0:T(8,128)(2,1)S(1)} %pad_maximum_fusion), channel_id=1, replica_groups=mesh['pts_0'=4,'pts_1'=16,'cand'=8] {'pts_1'}, dimensions={0}, use_global_device_ids=true | all-gather | bytes 2506752 | tf_op jit(solution)/shard_map/all_gather | solution.py:36
  60.5 0.6 fusion.24
  62.3 1.7 slice.44
  64.1 0.1 pad.5.clone
  64.2 2.4 %maximum_maximum_fusion = f16[264,4096]{1,0:T(8,128)(2,1)S(1)} fusion(f16[1,4096]{1,0:T(2,128)(2,1)S(1)} %bitcast.44, f16[1,4096]{1,0:T(2,128)(2,1)S(1)} %bitcast.43, f16[256,4096]{1,0:T(8,128)(2,1)} %slice.44, f16[264]{0:T(512)(128)(2,1)S(1)} %pad.5.clone), kind=kLoop, calls=%fused_computation.5 | loop fusion | flops 3244032 | bytes 4276752 | tf_op jit(solution)/shard_map/concatenate | solution.py:46
  66.6 68.2 %all-gather.3 = f16[1056,4096]{1,0:T(8,128)(2,1)} all-gather(f16[264,4096]{1,0:T(8,128)(2,1)S(1)} %maximum_maximum_fusion), channel_id=1, replica_groups=mesh['pts_0'=4,'pts_1'=16,'cand'=8] {'pts_0'}, dimensions={0}, use_global_device_ids=true | all-gather | bytes 10813440 | tf_op jit(solution)/shard_map/all_gather | solution.py:48
  134.9 9.8 %convert_element_type.11 = bf16[1056,4096]{1,0:T(8,128)(2,1)} convert(f16[1056,4096]{1,0:T(8,128)(2,1)} %all-gather.3) | non-fusion elementwise | flops 4325376 | bytes 17301504 | tf_op jit(solution)/shard_map/convert_element_type | solution.py:48
  146.0 0.9 dynamic-slice_bitcast_fusion.1
  146.9 3.5 %fusion.10 = f32[512,2]{0,1:T(2,128)S(1)} fusion(bf16[512,4096]{1,0:T(8,128)(2,1)} %param.5, bf16[1,4096]{1,0:T(2,128)(2,1)S(1)} %get-tuple-element.7, bf16[1,4096]{1,0:T(2,128)(2,1)S(1)} %get-tuple-element.6), kind=kOutput, calls=%fused_computation.11 | convolution fusion | flops 8422400 | bytes 4214784 | tf_op jit(solution)/shard_map/dot_general | solution.py:57
  150.5 0.6 fusion.21
  151.0 0.1 broadcast_select_fusion
  151.2 8.1 %fusion.5 = f32[4,256]{1,0:T(4,128)S(1)} fusion(bf16[512,4096]{1,0:T(8,128)(2,1)S(1)} %copy-done.1, bf16[4,264,4096]{2,1,0:T(8,128)(2,1)} %bitcast.41, f32[512,256]{0,1:T(8,128)S(1)} %broadcast_select_fusion, f32[512]{0:T(512)S(1)} %copy-done.3), kind=kOutput, calls=%fused_computation.9 | convolution fusion | flops 4297587712 | bytes 13113344 | tf_op jit(solution)/shard_map/dot_general | solution.py:70
  159.3 0.1 all_to_all.6
  159.3 23.6 %all_to_all.9 = f32[64,1,16]{2,1,0:T(1,128)S(1)} all-to-all(f32[64,1,16]{2,1,0:T(1,128)S(1)} %bitcast.42), channel_id=1, replica_groups=mesh['pts_0'=4,'pts_1'=16,'cand'=8] {'pts_0','pts_1'}, dimensions={0} | all-to-all | bytes 8192 | tf_op jit(solution)/shard_map/all_to_all | solution.py:79
  183.0 0.1 reduce_sum.19
  183.1 0.6 div.52
  (23 shorter events, 0.3 us)
Async XLA Ops:
  0.6 1.0 copy-start
  144.7 5.7 %copy-start.2 = (f32[512]{0:T(512)S(1)}, f32[512]{0:T(512)}, u32[]{:S(2)}) copy-start(f32[512]{0:T(512)} %param.7) | copy-start | bytes 6148
  146.9 4.3 %copy-start.1 = (bf16[512,4096]{1,0:T(8,128)(2,1)S(1)}, bf16[512,4096]{1,0:T(8,128)(2,1)}, u32[]{:S(2)}) copy-start(bf16[512,4096]{1,0:T(8,128)(2,1)} %param.5) | copy-start | bytes 12582916
  146.9 4.3 %copy-start.3 = (f32[512]{0:T(512)S(1)}, f32[512]{0:T(512)}, u32[]{:S(2)}) copy-start(f32[512]{0:T(512)} %param.6) | copy-start | bytes 6148
where the time goes:
time: 184 us
  blocking collectives  144 us (78%)
  matrix products  14.5 us (8%)
  other arithmetic  14 us (8%)
  between operations  5.85 us (3%)
  local copies, waits for them, and re-layouts  5.64 us (3%)
    all_gather x1, blocking collectives, body(): lax.all_gather(column, PTS[0], axis=0, tiled=True).astype(points.dtype)  68.2 us
    all_gather x1, blocking collectives, body(): along_z = lax.all_gather(sent, PTS[1], axis=0, tiled=True)  51.8 us
    all_to_all x1, blocking collectives, body(): part = lax.all_to_all(part.reshape(n_x * n_z, held), PTS, 0, 0, tiled=True)  23.6 us
    convert_element_type x1, other arithmetic, body(): lax.all_gather(column, PTS[0], axis=0, tiled=True).astype(points.dtype)  9.84 us
    dot_general x1, matrix products, body(): lax.dot_general(points, block[:, :n_z * held], (((1,), (2,)), ((), ())),...  8.08 us

commit v1 on v0

--- a/solution.py
+++ b/solution.py
@@ -45,7 +45,9 @@
     pad = jnp.zeros((8 - steps, width), jnp.float16)
     column = jnp.concatenate([along_z[:, :width], *chosen, pad], axis=0)
     column_rows = n_z * held + 8
-    block = lax.all_gather(column, PTS[0], axis=0, tiled=True).astype(points.dtype)
+    block = jnp.concatenate(
+        lax.all_to_all(jnp.stack([column] * lax.axis_size(PTS[0])), PTS[0], 0, 0), axis=0
+    ).astype(points.dtype)
     block = block.reshape(n_x, column_rows, width)
     chosen = jnp.concatenate(
         [

time: 184 us -> 209 us (1.14)
  waiting for transfers between devices: 0 us -> 86.4 us
  blocking collectives: 144 us -> 74.2 us
  starting transfers between devices: 0 us -> 5.68 us
  local copies, waits for them, and re-layouts: 5.64 us -> 10.2 us
  matrix products: 14.5 us -> 12.2 us
    all_to_all x0 -> x1, waiting for transfers between devices: none -> 86.4 us  [body(): lax.all_to_all(jnp.stack([column] * lax.axis_size(PTS[0])), PTS[0], 0, 0)]
    all_gather x1 -> x0, blocking collectives: 68.2 us -> none  [body(): lax.all_gather(column, PTS[0], axis=0, tiled=True).astype(points.dtype)]
    all_to_all x0 -> x1, starting transfers between devices: none -> 5.68 us  [body(): lax.all_to_all(jnp.stack([column] * lax.axis_size(PTS[0])), PTS[0], 0, 0)]
    another operation x0 -> x1, local copies, waits for them, and re-layouts: none -> 4.52 us  [body(): jnp.stack([column] * lax.axis_size(PTS[0]))]
    dot_general x1, matrix products: 3.52 us -> 1.18 us  [body(): lax.dot_general(points, chosen, (((1,), (1,)), ((), ())), preferred_eleme...]
  transfers between devices with their start and end apart: 0 -> 1, of which waited for: 0 -> 1; matrix products, arithmetic and copies ran while one was open for 0% -> 0% of each run, Pallas kernels for 0% -> 0%
where the time goes in v1:
time: 209 us
  waiting for transfers between devices  86.4 us (41%)
  blocking collectives  74.2 us (36%)
  other arithmetic  14.2 us (7%)
  matrix products  12.2 us (6%)
  local copies, waits for them, and re-layouts  10.2 us (5%)
  between operations  5.97 us (3%)
  starting transfers between devices  5.68 us (3%)
    all_to_all x1, waiting for transfers between devices, body(): lax.all_to_all(jnp.stack([column] * lax.axis_size(PTS[0])), PTS[0], 0, 0)  86.4 us
    all_gather x1, blocking collectives, body(): along_z = lax.all_gather(sent, PTS[1], axis=0, tiled=True)  51.8 us
    all_to_all x1, blocking collectives, body(): part = lax.all_to_all(part.reshape(n_x * n_z, held), PTS, 0, 0, tiled=True)  22.4 us
    convert_element_type x1, other arithmetic, body(): block = jnp.concatenate(lax.all_to_all(jnp.stack([column] * lax.axis_size...  10 us
    dot_general x1, matrix products, body(): lax.dot_general(points, block[:, :n_z * held], (((1,), (2,)), ((), ())),...  8.16 us
    all_to_all x1, starting transfers between devices, body(): lax.all_to_all(jnp.stack([column] * lax.axis_size(PTS[0])), PTS[0], 0, 0)  5.68 us
    another operation x1, local copies, waits for them, and re-layouts, body(): jnp.stack([column] * lax.axis_size(PTS[0]))  4.52 us
  transfers between devices with their start and end apart: 1, of which 1 were waited for; matrix products, arithmetic and copies ran while one was open for 0% of the time, Pallas kernels for 0%

profile of v1, /device:TPU:24, one launch (start us, length us, event | category | flops | bytes accessed | tf_op | source)
XLA Modules:
  0.0 208.9 jit_solution(4316902553373238681)
XLA Ops:
  0.7 0.7 and_select_fusion
  1.4 0.1 copy.9
  1.4 0.2 or_reduce_fusion
  1.6 0.6 gather_fusion
  2.4 0.1 reshape.152
  2.5 2.9 %convolution_convert_fusion = f16[18,4096]{1,0:T(8,128)(2,1)S(1)} fusion(bf16[512,4096]{1,0:T(8,128)(2,1)} %param.5, s32[18]{0:T(128)S(1)} %pad_add_fusion.1), kind=kOutput, calls=%fused_computation.3 | convolution fusion | flops 75598848 | bytes 4341832 | tf_op jit(solution)/shard_map/dot_general | solution.py:31
  5.5 51.8 %all-gather.1 = f16[256,4608]{1,0:T(8,128)(2,1)S(1)} all-gather(f16[16,4608]{1,0:T(8,128)(2,1)S(1)} %pad_maximum_fusion), channel_id=1, replica_groups=mesh['pts_0'=4,'pts_1'=16,'cand'=8] {'pts_1'}, dimensions={0}, use_global_device_ids=true | all-gather | bytes 2506752 | tf_op jit(solution)/shard_map/all_gather | solution.py:36
  57.4 0.6 fusion.24
  59.3 1.7 slice.44
  61.1 2.4 %maximum_maximum_fusion = f16[264,4096]{1,0:T(8,128)(2,1)S(1)} fusion(f16[1,4096]{1,0:T(2,128)(2,1)S(1)} %bitcast.41, f16[1,4096]{1,0:T(2,128)(2,1)S(1)} %bitcast.40, f16[256,4096]{1,0:T(8,128)(2,1)} %slice.44, f16[264]{0:T(512)(128)(2,1)S(1)} %pad.5.clone), kind=kLoop, calls=%fused_computation.5 | loop fusion | flops 3244032 | bytes 4276752 | tf_op jit(solution)/shard_map/concatenate | solution.py:46
  63.6 4.5 %stack.2 = f16[4,264,4096]{2,1,0:T(8,128)(2,1)} broadcast(f16[264,4096]{1,0:T(8,128)(2,1)S(1)} %maximum_maximum_fusion), dimensions={1,2} | broadcast | bytes 10813440 | tf_op jit(solution)/shard_map/stack | solution.py:49
  68.1 5.7 %all-to-all-start = ((f16[4,264,4096]{2,1,0:T(8,128)(2,1)}), f16[4,264,4096]{2,1,0:T(8,128)(2,1)}, u32[]{:S(2)}, u32[]{:S(2)}) async-start(f16[4,264,4096]{2,1,0:T(8,128)(2,1)} %stack.2), calls=%async_computation | async-start | bytes 17301504 | tf_op jit(solution)/shard_map/all_to_all | solution.py:49
  73.8 0.6 fusion.23
  78.3 86.4 %all-to-all-done = f16[4,264,4096]{2,1,0:T(8,128)(2,1)} async-done(((f16[4,264,4096]{2,1,0:T(8,128)(2,1)}), f16[4,264,4096]{2,1,0:T(8,128)(2,1)}, u32[]{:S(2)}, u32[]{:S(2)}) %all-to-all-start) | async-done | bytes 8650784 | tf_op jit(solution)/shard_map/all_to_all | solution.py:49
  164.6 10.0 %convert_element_type.12 = bf16[4,264,4096]{2,1,0:T(8,128)(2,1)} convert(f16[4,264,4096]{2,1,0:T(8,128)(2,1)} %all-to-all-done) | non-fusion elementwise | flops 4325376 | bytes 17301504 | tf_op jit(solution)/shard_map/convert_element_type | solution.py:50
  174.7 0.9 dynamic-slice_bitcast_fusion.1
  175.6 1.2 fusion.10
  176.8 0.6 fusion.21
  177.4 0.1 broadcast_select_fusion
  177.5 8.2 %fusion.5 = f32[4,256]{1,0:T(4,128)S(1)} fusion(bf16[512,4096]{1,0:T(8,128)(2,1)S(1)} %copy-done.1, bf16[4,264,4096]{2,1,0:T(8,128)(2,1)} %convert_element_type.12, f32[512,256]{0,1:T(8,128)S(1)} %broadcast_select_fusion, f32[512]{0:T(512)S(1)} %copy-done.3), kind=kOutput, calls=%fused_computation.9 | convolution fusion | flops 4297587712 | bytes 13113344 | tf_op jit(solution)/shard_map/dot_general | solution.py:72
  185.7 0.1 all_to_all.10
  185.7 22.4 %all_to_all.14 = f32[64,1,16]{2,1,0:T(1,128)S(1)} all-to-all(f32[64,1,16]{2,1,0:T(1,128)S(1)} %bitcast.39), channel_id=1, replica_groups=mesh['pts_0'=4,'pts_1'=16,'cand'=8] {'pts_0','pts_1'}, dimensions={0} | all-to-all | bytes 8192 | tf_op jit(solution)/shard_map/all_to_all | solution.py:81
  208.2 0.1 reduce_sum.19
  208.2 0.6 div.52
  (25 shorter events, 0.5 us)
Async XLA Ops:
  0.6 1.0 copy-start
  68.1 96.6 %all-to-all-start = ((f16[4,264,4096]{2,1,0:T(8,128)(2,1)}), f16[4,264,4096]{2,1,0:T(8,128)(2,1)}, u32[]{:S(2)}, u32[]{:S(2)}) async-start(f16[4,264,4096]{2,1,0:T(8,128)(2,1)} %stack.2), calls=%async_computation | async-start | bytes 17301504 | tf_op jit(solution)/shard_map/all_to_all | solution.py:49
  164.6 10.9 %copy-start.1 = (bf16[512,4096]{1,0:T(8,128)(2,1)S(1)}, bf16[512,4096]{1,0:T(8,128)(2,1)}, u32[]{:S(2)}) copy-start(bf16[512,4096]{1,0:T(8,128)(2,1)} %param.5) | copy-start | bytes 12582916
  174.7 2.1 %copy-start.2 = (f32[512]{0:T(512)S(1)}, f32[512]{0:T(512)}, u32[]{:S(2)}) copy-start(f32[512]{0:T(512)} %param.7) | copy-start | bytes 6148
  175.6 1.9 copy-start.3
